TPU v7x, 32 devices: a whole 2x2x4 slice. The times are simulated.
32 devices in a mesh: tm: 8 (over z, x), exp: 4 (over y, core).
Axes of the slice: x: 2, y: 2, z: 4, core: 2. Of those that a mesh axis runs over, the one named last changes fastest.
Arguments:
- transitions: float32 [512, 256, 256], P('tm'), may hold values from -0.2 to 1.2
- pattern: int32 [512, 4, 4], P('tm'), may hold values from 0 to 1, as said below
- obs_mask: int32 [4, 512, 256], P('exp', 'tm'), may hold values 0 or 1
- measured: float32 [4, 512, 256], P('exp', 'tm'), may hold values from -6 to 6
- prior_mean: float32 [4, 256], P('exp'), may hold values from -6 to 6
- filter_gain: float32 [256], replicated, may hold values from 0 to 0.6
- smooth_gain: float32 [256], replicated, may hold values from 0.3 to 1
Outputs:
- smoothed: float32 [4, 512, 256], P('exp', 'tm')
- information: float32 [256, 256], replicated
Inputs may be any that keep to these rules, and one draw needn't show every extreme that they name: `pattern`: diagonal blocks are always present.
All inputs are finite; a program needn't handle non-finite values. No bound on the sum of `obs_mask` on one device may be relied on, other than what follows from the above.
Results may differ from a plain program's by a relative error of at most 0.0001.
Values sent between devices are 32-bit elements; how exact they have to be, the bound alone decides.
A program may use at most 192 MiB of HBM per device.

v0:
```python
import jax
import jax.numpy as jnp
from jax import lax
from jax.sharding import PartitionSpec as P


def entering(x, axis, combine, identity, reverse):
    length, index = (lax.axis_size(axis), lax.axis_index(axis))
    everything = jax.tree.map(lambda part: lax.all_gather(part, axis), x)
    start = jax.tree.map(
        lambda part, zero: jnp.broadcast_to(jnp.asarray(zero, part.dtype), part.shape), x, identity
    )

    def hop(k, before):
        at = length - 1 - k if reverse else k
        reached = at > index if reverse else at < index
        new = combine(before, jax.tree.map(lambda part: part[at], everything))
        return jax.tree.map(lambda a, b: jnp.where(reached, a, b), new, before)

    return lax.fori_loop(0, length, hop, start)


def masked_dense(transitions, pattern):
    count_steps, state_width, _ = transitions.shape
    block_count = pattern.shape[1]
    block_size = state_width // block_count
    reshaped = transitions.reshape(count_steps, block_count, block_size, block_count, block_size)
    weights = pattern.astype(jnp.float32)[:, :, None, :, None]
    return (reshaped * weights).reshape(count_steps, state_width, state_width)


def chain_product(matrices):
    while matrices.shape[0] > 1:
        paired = matrices.shape[0] // 2 * 2
        earlier_maps = matrices[0:paired:2]
        later_maps = matrices[1:paired:2]
        joined = jnp.einsum(
            "bij,bjk->bik", later_maps, earlier_maps, precision=lax.Precision.HIGHEST
        )
        matrices = joined
    return matrices[0]


def compose(earlier_maps, later_maps):
    highest = lax.Precision.HIGHEST
    return (
        jnp.dot(later_maps[0], earlier_maps[0], precision=highest),
        jnp.dot(later_maps[0], earlier_maps[1], precision=highest) + later_maps[1],
    )


def run_filter(dense_steps, keep_rows, drive_terms, start_state):

    def update(state, inputs):
        trans_step, keep_step, drive_step = inputs
        predict = jnp.dot(trans_step, state, precision=lax.Precision.HIGHEST)
        state = keep_step * predict + drive_step
        return (state, (state, predict))

    last_state, (filtered, predicted) = lax.scan(
        update, start_state, (dense_steps, keep_rows, drive_terms)
    )
    return (last_state, filtered, predicted)


def run_smoother(dense_steps, filtered, predicted, smooth_gain, carried_in):

    def update(carried, inputs):
        trans_step, state, predict = inputs
        smooth_now = state + smooth_gain * carried
        residual = smooth_now - predict
        carried = jnp.dot(residual, trans_step, precision=lax.Precision.HIGHEST)
        return (carried, (smooth_now, residual))

    first_carry, (smoothed, residuals) = lax.scan(
        update, carried_in, (dense_steps, filtered, predicted), reverse=True
    )
    return (first_carry, smoothed, residuals)


def shards(transitions, pattern, obs_mask, measured, prior_mean, filter_gain, smooth_gain):
    highest = lax.Precision.HIGHEST
    dense_steps = masked_dense(transitions, pattern)
    state_width = dense_steps.shape[1]
    count_steps = dense_steps.shape[0]
    mask_rows = obs_mask[0].astype(jnp.float32)
    keep_rows = 1.0 - filter_gain[None, :] * mask_rows
    drive_terms = filter_gain[None, :] * mask_rows * measured[0]
    filter_map = chain_product(keep_rows[:, :, None] * dense_steps)
    smoother_map = chain_product(smooth_gain[None, :, None] * dense_steps).T
    zero_vector = jnp.zeros((state_width,), jnp.float32)
    filter_shift, _, _ = run_filter(dense_steps, keep_rows, drive_terms, zero_vector)
    prior_state = prior_mean[0]
    identity = jnp.eye(state_width, dtype=jnp.float32)
    prefix_maps = entering(
        (filter_map, filter_shift), "tm", compose, (identity, zero_vector), False
    )
    start_state = jnp.dot(prefix_maps[0], prior_state, precision=highest) + prefix_maps[1]
    _, filtered, predicted = run_filter(dense_steps, keep_rows, drive_terms, start_state)
    smoother_shift, _, _ = run_smoother(dense_steps, filtered, predicted, smooth_gain, zero_vector)
    suffix_maps = entering(
        (smoother_map, smoother_shift), "tm", compose, (identity, zero_vector), True
    )
    carried_in = suffix_maps[1]
    _, smoothed, residuals = run_smoother(dense_steps, filtered, predicted, smooth_gain, carried_in)
    local_info = jnp.dot(residuals.T, residuals, precision=highest)
    total_info = lax.psum(local_info, ("tm", "exp"))
    information = total_info / (count_steps * lax.axis_size("tm") * lax.axis_size("exp"))
    return (smoothed[None], information)


def solution(mesh):
    in_specs = (
        P("tm", None, None),
        P("tm", None, None),
        P("exp", "tm", None),
        P("exp", "tm", None),
        P("exp", None),
        P(),
        P(),
    )
    out_specs = (P("exp", "tm", None), P())
    return jax.shard_map(shards, mesh=mesh, in_specs=in_specs, out_specs=out_specs, check_vma=False)
```

profile of v0, /device:TPU:0, one launch (start us, length us, event | category | flops | bytes accessed | tf_op | source)
XLA Modules:
  0.0 665.8 jit_solution(17805602499832563561)
XLA Ops:
  8.1 11.2 %mul.71 = f32[64,4,64,4,64]{4,3,2,1,0:T(4,128)} broadcast(f32[64,4,4]{2,1,0:T(4,128)S(1)} %copy.10), dimensions={0,1,3} | broadcast | bytes 16781312 | tf_op jit(solution)/shard_map/mul | solution.py:29
  19.3 30.5 %mul.72 = f32[64,256,256]{2,1,0:T(8,128)} reshape(f32[64,4,64,4,64]{4,3,2,1,0:T(4,128)} %mul.71) | data formatting | bytes 33554432 | tf_op jit(solution)/shard_map/mul | solution.py:29
  49.8 17.7 %broadcast_multiply_fusion = (f32[64,256,256]{2,1,0:T(8,128)S(1)}, f32[64,256,256]{2,1,0:T(8,128)}) fusion(f32[64,256]{1,0:T(8,128)S(1)} %get-tuple-element.1043, f32[64,256,256]{2,1,0:T(8,128)} %param.19, f32[64,256,256]{2,1,0:T(8,128)} %mul.72), kind=kLoop, calls=%fused_computation.50 | loop fusion | flops 8388608 | bytes 67174400 | tf_op jit(solution)/shard_map/mul | solution.py:89
  67.6 10.7 %fusion.27 = f32[32,256,256]{2,1,0:T(8,128)} fusion(f32[64,256,256]{2,1,0:T(8,128)S(1)} %get-tuple-element.734), kind=kOutput, calls=%fused_computation.47 | convolution fusion | flops 6442450944 | bytes 25165824 | tf_op jit(solution)/shard_map/bij,bjk->bik/dot_general | solution.py:37
  78.2 8.4 %fusion.33 = f32[16,256,256]{2,1,0:T(8,128)S(1)} fusion(f32[32,256,256]{2,1,0:T(8,128)} %fusion.27), kind=kOutput, calls=%fused_computation.55 | convolution fusion | flops 3221225472 | bytes 12582912 | tf_op jit(solution)/shard_map/bij,bjk->bik/dot_general | solution.py:37
  86.7 2.2 fusion.39
  91.9 7.3 %broadcast_multiply_fusion.1 = f32[64,256,256]{2,1,0:T(8,128)S(1)} fusion(f32[64,256,256]{2,1,0:T(8,128)} %get-tuple-element.1124, f32[256]{0:T(256)S(1)} %copy-done.1), kind=kLoop, calls=%fused_computation.54 | loop fusion | flops 4194304 | bytes 33555456 | tf_op jit(solution)/shard_map/mul | solution.py:90
  99.1 10.7 %fusion.30 = f32[32,256,256]{2,1,0:T(8,128)} fusion(f32[64,256,256]{2,1,0:T(8,128)S(1)} %broadcast_multiply_fusion.1), kind=kOutput, calls=%fused_computation.51 | convolution fusion | flops 6442450944 | bytes 25165824 | tf_op jit(solution)/shard_map/bij,bjk->bik/dot_general | solution.py:37
  109.8 8.5 %fusion.36 = f32[16,256,256]{2,1,0:T(8,128)S(1)} fusion(f32[32,256,256]{2,1,0:T(8,128)} %fusion.30), kind=kOutput, calls=%fused_computation.58 | convolution fusion | flops 3221225472 | bytes 12582912 | tf_op jit(solution)/shard_map/bij,bjk->bik/dot_general | solution.py:37
  118.3 2.2 fusion.42
  122.3 1.3 fusion.58
  123.8 85.5 %while.92 = (s32[]{:T(128)}, f32[256]{0:T(256)S(1)}, f32[64,256]{1,0:T(8,128)S(1)}, f32[64,256,256]{2,1,0:T(8,128)}, f32[64,256]{1,0:T(8,128)S(1)}, /*index=5*/s32[]{:T(128)}, s32[]{:T(128)}) while((s32[]{:T(128)}, f32[256]{0:T(256)S(1)}, f32[64,256]{1,0:T(8,128)S(1)}, f32[64,256,256]{2,1,0:T(8,128)}, f32[64,256]{1,0:T(8,128)S(1)}, ...), condition=%wide.region_1.2_spmd.clone, body=%wide.region_0.1_spmd.clone.sunk | while | flops 787203 | bytes 275035 | solution.py:60
  127.8 1.2 fusion.108
  130.5 1.2 fusion.108
  131.8 1.2 fusion.108
  133.1 1.2 fusion.108
  138.5 1.2 fusion.108
  139.8 1.2 fusion.108
  141.1 1.2 fusion.108
  142.5 1.3 fusion.108
  147.8 1.3 fusion.108
  149.1 1.3 fusion.108
  150.5 1.2 fusion.108
  151.8 1.2 fusion.108
  153.2 1.2 fusion.108
  157.2 1.2 fusion.108
  158.5 1.2 fusion.108
  159.8 1.2 fusion.108
  161.2 1.2 fusion.108
  162.5 1.2 fusion.108
  163.8 1.2 fusion.108
  165.2 1.3 fusion.108
  166.5 1.3 fusion.108
  167.9 1.3 fusion.108
  169.2 1.3 fusion.108
  170.5 1.2 fusion.108
  171.9 1.2 fusion.108
  173.2 1.2 fusion.108
  174.5 1.2 fusion.108
  179.9 1.2 fusion.108
  181.2 1.2 fusion.108
  182.5 1.2 fusion.108
  187.9 1.2 fusion.108
  189.2 1.2 fusion.108
  190.5 1.2 fusion.108
  195.9 1.2 fusion.108
  197.2 1.2 fusion.108
  209.2 22.2 %all-gather.4 = f32[8,1,256]{2,1,0:T(1,128)S(1)} all-gather(f32[1,1,256]{2,1,0:T(1,128)S(1)} %bitcast.198), channel_id=4, replica_groups=mesh['tm'=8,'exp'=4] {'tm'}, dimensions={0}, use_global_device_ids=true | all-gather | bytes 9216 | tf_op jit(solution)/shard_map/all_gather | solution.py:9
  231.5 21.6 %while.93 = (s32[]{:T(128)}, f32[256,256]{1,0:T(8,128)S(1)}, f32[256]{0:T(256)S(1)}, s32[]{:T(128)}, f32[8,256,256]{2,1,0:T(8,128)}, /*index=5*/f32[8,256]{1,0:T(8,128)S(1)}, s32[]{:T(128)}, s32[]{:T(128)}) while((s32[]{:T(128)}, f32[256,256]{1,0:T(8,128)S(1)}, f32[256]{0:T(256)S(1)}, s32[]{:T(128)}, f32[8,256,256]{2,1,0:T(8,128)}, ...), condition=%wide.region_3.4_spmd.clone, body=%wide.region_2.3_spmd.clone.sunk | while | flops 202179584 | bytes 1846383 | solution.py:20
  232.8 1.3 convolution_select_fusion.2
  235.5 1.3 convolution_select_fusion.2
  238.2 1.3 convolution_select_fusion.2
  240.9 1.3 convolution_select_fusion.2
  243.6 1.3 convolution_select_fusion.2
  246.3 1.3 convolution_select_fusion.2
  249.0 1.3 convolution_select_fusion.2
  251.7 1.3 convolution_select_fusion.2
  253.5 90.9 %while.89 = (s32[]{:T(128)}, f32[256]{0:T(256)S(1)}, f32[64,256]{1,0:T(8,128)S(1)}, f32[64,256]{1,0:T(8,128)S(1)}, f32[64,256]{1,0:T(8,128)S(1)}, /*index=5*/f32...) while((s32[]{:T(128)}, f32[256]{0:T(256)S(1)}, f32[64,256]{1,0:T(8,128)S(1)}, ...), condition=%wide.region_5.6_spmd, body=%wide.region_4.5_spmd.sunk | while | flops 786946 | bytes 277097 | solution.py:60
  344.4 77.4 %while.90 = (s32[]{:T(128)}, f32[256]{0:T(256)S(1)}, f32[64,256]{1,0:T(8,128)S(1)}, f32[256]{0:T(256)S(1)}, f32[64,256]{1,0:T(8,128)S(1)}, /*index=5*/f32[64,256,256]{2,1,0:T(8,128)}, s32[]{:T(128)}, s32[]{:T(128)}) while((s32[]{:T(128)}, f32[256]{0:T(256)S(1)}, f32[64,256]{1,0:T(8,128)S(1)}, f32[256]{0:T(256)S(1)}, f32[64,256]{1,0:T(8,128)S(1)}, ...), condition=%wide.region_7.8_spmd, body=%wide.region_6.7_spmd.sunk | while | flops 787203 | bytes 273513 | solution.py:75
  421.8 16.3 %all-gather.5 = f32[8,1,256]{2,1,0:T(1,128)S(1)} all-gather(f32[1,1,256]{2,1,0:T(1,128)S(1)} %bitcast.197), channel_id=5, replica_groups=mesh['tm'=8,'exp'=4] {'tm'}, dimensions={0}, use_global_device_ids=true | all-gather | bytes 9216 | tf_op jit(solution)/shard_map/all_gather | solution.py:9
  438.1 10.8 %while.94 = (s32[]{:T(128)}, f32[256]{0:T(256)S(1)}, s32[]{:T(128)}, f32[8,256,256]{2,1,0:T(8,128)}, f32[8,256]{1,0:T(8,128)S(1)}, /*index=5*/s32[]{:T(128)}, s32[]{:T(128)}, s32[]{:T(128)}, s32[]{:T(128)}) while((s32[]{:T(128)}, f32[256]{0:T(256)S(1)}, s32[]{:T(128)}, f32[8,256,256]{2,1,0:T(8,128)}, f32[8,256]{1,0:T(8,128)S(1)}, ...), condition=%wide.region_9.10_spmd.clone, body=%wide.region_8.9_spmd.clone.sunk | while | flops 787464 | bytes 272552 | solution.py:20
  448.9 83.7 %while.91 = (s32[]{:T(128)}, f32[256]{0:T(256)S(1)}, f32[64,256]{1,0:T(8,128)S(1)}, f32[64,256]{1,0:T(8,128)S(1)}, f32[64,256]{1,0:T(8,128)S(1)}, /*index=5*/f32...) while((s32[]{:T(128)}, f32[256]{0:T(256)S(1)}, ...), condition=%wide.region_11.12_spmd, body=%wide.region_10.11_spmd.sunk | while | flops 787203 | bytes 278665 | solution.py:75
  533.7 123.9 %all-reduce.2.cloned.1.call-done = f32[256,256]{1,0:T(8,128)} async-done(((f32[256,256]{1,0:T(8,128)}), f32[256,256]{1,0:T(8,128)}) %all-reduce.2.cloned.1.call-update) | async-done | bytes 262160 | tf_op jit(solution)/shard_map/psum | solution.py:107
  657.6 1.7 broadcast_multiply_fusion.2
  (1167 shorter events, 313.4 us)
Async XLA Ops:
  7.2 245.9 %copy-start = (f32[1,256]{1,0:T(1,128)S(1)}, f32[1,256]{1,0:T(1,128)}, u32[]{:S(2)}) copy-start(f32[1,256]{1,0:T(1,128)} %param.23) | copy-start | bytes 3076
  7.2 224.3 %all-gather.11.cloned.1.call-start = ((), (), s32[]{:S(2)}) async-start(), calls=%async_computation.2 | async-start | bytes 2359296 | tf_op jit(solution)/shard_map/all_gather | solution.py:9
  19.3 30.5 %copy-start.3 = (f32[1,64,256]{2,1,0:T(8,128)S(1)}, f32[1,64,256]{2,1,0:T(8,128)}, u32[]{:S(2)}) copy-start(f32[1,64,256]{2,1,0:T(8,128)} %param.22) | copy-start | bytes 196612
  19.3 30.5 %copy-start.4 = (s32[1,64,256]{2,1,0:T(8,128)S(1)}, s32[1,64,256]{2,1,0:T(8,128)}, u32[]{:S(2)}) copy-start(s32[1,64,256]{2,1,0:T(8,128)} %param.21) | copy-start | bytes 196612
  19.3 30.5 %copy-start.5 = (f32[256]{0:T(256)S(1)}, f32[256]{0:T(256)}, u32[]{:S(2)}) copy-start(f32[256]{0:T(256)} %param.24) | copy-start | bytes 3076
  86.6 5.2 copy-start.1
  91.8 346.3 %all-gather.9.cloned.1.call-start = ((), (), s32[]{:S(2)}) async-start(), calls=%async_computation.1 | async-start | bytes 2359296 | tf_op jit(solution)/shard_map/all_gather | solution.py:9
  123.6 534.0 %all-reduce.2.cloned.1.call-start = ((), (), s32[]{:S(2)}) async-start(), calls=%async_computation | async-start | bytes 524288 | tf_op jit(solution)/shard_map/psum | solution.py:107
  532.6 126.7 %copy-start.2 = (f32[64,256]{1,0:T(8,128)}, f32[64,256]{1,0:T(8,128)S(1)}, u32[]{:S(2)}) copy-start(f32[64,256]{1,0:T(8,128)S(1)} %get-tuple-element.599) | copy-start | bytes 196612
Sparse Core Ops, SparseCore 0:
  91.9 52.1 all-gather.10
  146.8 47.8 all-gather.8
  533.9 123.7 all-reduce.1
where the time goes:
time: 676 us; the launch traced here: 666 us
  matrix products  383 us (57%)
  waiting for transfers between devices  124 us (18%)
  local copies, waits for them, and re-layouts  63 us (9%)
  blocking collectives  38.6 us (6%)
  other arithmetic  33 us (5%)
  between operations  14 us (2%)
  loops' own time  9.82 us (1%)
    dot_general x128, matrix products, update(): predict = jnp.dot(trans_step, state, precision=lax.Precision.HIGHEST)  157 us
    dot_general x128, matrix products, update(): carried = jnp.dot(residual, trans_step, precision=lax.Precision.HIGHEST)  146 us
    psum x1, waiting for transfers between devices, shards(): total_info = lax.psum(local_info, ('tm', 'exp'))  124 us
    dot_general x12, matrix products, chain_product(): jnp.einsum('bij,bjk->bik', later_maps, earlier_maps, precision=lax.Precis...  48.6 us
    mul x2, local copies, waits for them, and re-layouts, masked_dense(): return (reshaped * weights).reshape(count_steps, state_width, state_width)  41.7 us
    all_gather x2, blocking collectives, entering(): everything = jax.tree.map(lambda part: lax.all_gather(part, axis), x)  38.6 us
    dot_general x16, matrix products, compose(): jnp.dot(later_maps[0], earlier_maps[1], precision=highest) + later_maps[1]  19.6 us
    mul x1, other arithmetic, shards(): filter_map = chain_product(keep_rows[:, :, None] * dense_steps)  17.7 us
  transfers between devices with their start and end apart: 3, of which 1 were waited for; matrix products, arithmetic and copies ran while one was open for 45% of the time, Pallas kernels for 0%

commit v1 on v0

--- a/solution.py
+++ b/solution.py
@@ -2,6 +2,7 @@
 import jax.numpy as jnp
 from jax import lax
 from jax.sharding import PartitionSpec as P
+from jax.lax import all_gather
 
 
 def entering(x, axis, combine, identity, reverse):
@@ -104,7 +105,8 @@
     carried_in = suffix_maps[1]
     _, smoothed, residuals = run_smoother(dense_steps, filtered, predicted, smooth_gain, carried_in)
     local_info = jnp.dot(residuals.T, residuals, precision=highest)
-    total_info = lax.psum(local_info, ("tm", "exp"))
+    w2 = all_gather(local_info, ("tm", "exp"))
+    total_info = jnp.sum(w2, 0)
     information = total_info / (count_steps * lax.axis_size("tm") * lax.axis_size("exp"))
     return (smoothed[None], information)
 

time: 676 us -> 631 us (0.933)
  waiting for transfers between devices: 124 us -> 76.5 us
    psum x1 -> x0, waiting for transfers between devices: 124 us -> none  [shards(): total_info = lax.psum(local_info, ('tm', 'exp'))]
    all_gather x0 -> x1, waiting for transfers between devices: none -> 76.5 us  [shards(): w2 = all_gather(local_info, ('tm', 'exp'))]
  transfers between devices with their start and end apart: 3 -> 3, of which waited for: 1 -> 1; matrix products, arithmetic and copies ran while one was open for 45% -> 48% of each run, Pallas kernels for 0% -> 0%
where the time goes in v1:
time: 631 us; the launch traced here: 621 us
  matrix products  383 us (61%)
  waiting for transfers between devices  76.5 us (12%)
  local copies, waits for them, and re-layouts  63 us (10%)
  blocking collectives  38.6 us (6%)
  other arithmetic  36 us (6%)
  between operations  14 us (2%)
  loops' own time  9.82 us (2%)
    dot_general x128, matrix products, update(): predict = jnp.dot(trans_step, state, precision=lax.Precision.HIGHEST)  157 us
    dot_general x128, matrix products, update(): carried = jnp.dot(residual, trans_step, precision=lax.Precision.HIGHEST)  146 us
    all_gather x1, waiting for transfers between devices, shards(): w2 = all_gather(local_info, ('tm', 'exp'))  76.5 us
    dot_general x12, matrix products, chain_product(): jnp.einsum('bij,bjk->bik', later_maps, earlier_maps, precision=lax.Precis...  48.6 us
    mul x2, local copies, waits for them, and re-layouts, masked_dense(): return (reshaped * weights).reshape(count_steps, state_width, state_width)  41.7 us
    all_gather x2, blocking collectives, entering(): everything = jax.tree.map(lambda part: lax.all_gather(part, axis), x)  38.6 us
    dot_general x16, matrix products, compose(): jnp.dot(later_maps[0], earlier_maps[1], precision=highest) + later_maps[1]  19.6 us
    mul x1, other arithmetic, shards(): filter_map = chain_product(keep_rows[:, :, None] * dense_steps)  17.7 us
  transfers between devices with their start and end apart: 3, of which 1 were waited for; matrix products, arithmetic and copies ran while one was open for 48% of the time, Pallas kernels for 0%

profile of v1, /device:TPU:0, one launch (start us, length us, event | category | flops | bytes accessed | tf_op | source)
XLA Modules:
  0.0 621.4 jit_solution(11062786701597148592)
XLA Ops:
  8.1 11.2 %mul.71 = f32[64,4,64,4,64]{4,3,2,1,0:T(4,128)} broadcast(f32[64,4,4]{2,1,0:T(4,128)S(1)} %copy.10), dimensions={0,1,3} | broadcast | bytes 16781312 | tf_op jit(solution)/shard_map/mul | solution.py:30
  19.3 30.5 %mul.72 = f32[64,256,256]{2,1,0:T(8,128)} reshape(f32[64,4,64,4,64]{4,3,2,1,0:T(4,128)} %mul.71) | data formatting | bytes 33554432 | tf_op jit(solution)/shard_map/mul | solution.py:30
  49.8 17.7 %broadcast_multiply_fusion = (f32[64,256,256]{2,1,0:T(8,128)S(1)}, f32[64,256,256]{2,1,0:T(8,128)}) fusion(f32[64,256]{1,0:T(8,128)S(1)} %get-tuple-element.1043, f32[64,256,256]{2,1,0:T(8,128)} %param.19, f32[64,256,256]{2,1,0:T(8,128)} %mul.72), kind=kLoop, calls=%fused_computation.50 | loop fusion | flops 8388608 | bytes 67174400 | tf_op jit(solution)/shard_map/mul | solution.py:90
  67.6 10.7 %fusion.27 = f32[32,256,256]{2,1,0:T(8,128)} fusion(f32[64,256,256]{2,1,0:T(8,128)S(1)} %get-tuple-element.734), kind=kOutput, calls=%fused_computation.47 | convolution fusion | flops 6442450944 | bytes 25165824 | tf_op jit(solution)/shard_map/bij,bjk->bik/dot_general | solution.py:38
  78.2 8.4 %fusion.33 = f32[16,256,256]{2,1,0:T(8,128)S(1)} fusion(f32[32,256,256]{2,1,0:T(8,128)} %fusion.27), kind=kOutput, calls=%fused_computation.55 | convolution fusion | flops 3221225472 | bytes 12582912 | tf_op jit(solution)/shard_map/bij,bjk->bik/dot_general | solution.py:38
  86.7 2.2 fusion.39
  91.9 7.3 %broadcast_multiply_fusion.1 = f32[64,256,256]{2,1,0:T(8,128)S(1)} fusion(f32[64,256,256]{2,1,0:T(8,128)} %get-tuple-element.1124, f32[256]{0:T(256)S(1)} %copy-done.1), kind=kLoop, calls=%fused_computation.54 | loop fusion | flops 4194304 | bytes 33555456 | tf_op jit(solution)/shard_map/mul | solution.py:91
  99.1 10.7 %fusion.30 = f32[32,256,256]{2,1,0:T(8,128)} fusion(f32[64,256,256]{2,1,0:T(8,128)S(1)} %broadcast_multiply_fusion.1), kind=kOutput, calls=%fused_computation.51 | convolution fusion | flops 6442450944 | bytes 25165824 | tf_op jit(solution)/shard_map/bij,bjk->bik/dot_general | solution.py:38
  109.8 8.5 %fusion.36 = f32[16,256,256]{2,1,0:T(8,128)S(1)} fusion(f32[32,256,256]{2,1,0:T(8,128)} %fusion.30), kind=kOutput, calls=%fused_computation.58 | convolution fusion | flops 3221225472 | bytes 12582912 | tf_op jit(solution)/shard_map/bij,bjk->bik/dot_general | solution.py:38
  118.3 2.2 fusion.42
  122.3 1.3 fusion.58
  123.8 85.5 %while.92 = (s32[]{:T(128)}, f32[256]{0:T(256)S(1)}, f32[64,256]{1,0:T(8,128)S(1)}, f32[64,256,256]{2,1,0:T(8,128)}, f32[64,256]{1,0:T(8,128)S(1)}, /*index=5*/s32[]{:T(128)}, s32[]{:T(128)}) while((s32[]{:T(128)}, f32[256]{0:T(256)S(1)}, f32[64,256]{1,0:T(8,128)S(1)}, f32[64,256,256]{2,1,0:T(8,128)}, f32[64,256]{1,0:T(8,128)S(1)}, ...), condition=%wide.region_1.2_spmd.clone, body=%wide.region_0.1_spmd.clone.sunk | while | flops 787203 | bytes 275035 | solution.py:61
  127.8 1.2 fusion.108
  130.5 1.2 fusion.108
  131.8 1.2 fusion.108
  133.1 1.2 fusion.108
  138.5 1.2 fusion.108
  139.8 1.2 fusion.108
  141.1 1.2 fusion.108
  142.5 1.3 fusion.108
  147.8 1.3 fusion.108
  149.1 1.3 fusion.108
  150.5 1.2 fusion.108
  151.8 1.2 fusion.108
  153.2 1.2 fusion.108
  157.2 1.2 fusion.108
  158.5 1.2 fusion.108
  159.8 1.2 fusion.108
  161.2 1.2 fusion.108
  162.5 1.2 fusion.108
  163.8 1.2 fusion.108
  165.2 1.3 fusion.108
  166.5 1.3 fusion.108
  167.9 1.3 fusion.108
  169.2 1.3 fusion.108
  170.5 1.2 fusion.108
  171.9 1.2 fusion.108
  173.2 1.2 fusion.108
  174.5 1.2 fusion.108
  179.9 1.2 fusion.108
  181.2 1.2 fusion.108
  182.5 1.2 fusion.108
  187.9 1.2 fusion.108
  189.2 1.2 fusion.108
  190.5 1.2 fusion.108
  195.9 1.2 fusion.108
  197.2 1.2 fusion.108
  209.2 22.2 %all-gather.5 = f32[8,1,256]{2,1,0:T(1,128)S(1)} all-gather(f32[1,1,256]{2,1,0:T(1,128)S(1)} %bitcast.200), channel_id=4, replica_groups=mesh['tm'=8,'exp'=4] {'tm'}, dimensions={0}, use_global_device_ids=true | all-gather | bytes 9216 | tf_op jit(solution)/shard_map/all_gather | solution.py:10
  231.5 21.6 %while.93 = (s32[]{:T(128)}, f32[256,256]{1,0:T(8,128)S(1)}, f32[256]{0:T(256)S(1)}, s32[]{:T(128)}, f32[8,256,256]{2,1,0:T(8,128)}, /*index=5*/f32[8,256]{1,0:T(8,128)S(1)}, s32[]{:T(128)}, s32[]{:T(128)}) while((s32[]{:T(128)}, f32[256,256]{1,0:T(8,128)S(1)}, f32[256]{0:T(256)S(1)}, s32[]{:T(128)}, f32[8,256,256]{2,1,0:T(8,128)}, ...), condition=%wide.region_3.4_spmd.clone, body=%wide.region_2.3_spmd.clone.sunk | while | flops 202179584 | bytes 1846383 | solution.py:21
  232.8 1.3 convolution_select_fusion.2
  235.5 1.3 convolution_select_fusion.2
  238.2 1.3 convolution_select_fusion.2
  240.9 1.3 convolution_select_fusion.2
  243.6 1.3 convolution_select_fusion.2
  246.3 1.3 convolution_select_fusion.2
  249.0 1.3 convolution_select_fusion.2
  251.7 1.3 convolution_select_fusion.2
  253.5 90.9 %while.89 = (s32[]{:T(128)}, f32[256]{0:T(256)S(1)}, f32[64,256]{1,0:T(8,128)S(1)}, f32[64,256]{1,0:T(8,128)S(1)}, f32[64,256]{1,0:T(8,128)S(1)}, /*index=5*/f32...) while((s32[]{:T(128)}, f32[256]{0:T(256)S(1)}, f32[64,256]{1,0:T(8,128)S(1)}, ...), condition=%wide.region_5.6_spmd, body=%wide.region_4.5_spmd.sunk | while | flops 786946 | bytes 277097 | solution.py:61
  344.4 77.4 %while.90 = (s32[]{:T(128)}, f32[256]{0:T(256)S(1)}, f32[64,256]{1,0:T(8,128)S(1)}, f32[256]{0:T(256)S(1)}, f32[64,256]{1,0:T(8,128)S(1)}, /*index=5*/f32[64,256,256]{2,1,0:T(8,128)}, s32[]{:T(128)}, s32[]{:T(128)}) while((s32[]{:T(128)}, f32[256]{0:T(256)S(1)}, f32[64,256]{1,0:T(8,128)S(1)}, f32[256]{0:T(256)S(1)}, f32[64,256]{1,0:T(8,128)S(1)}, ...), condition=%wide.region_7.8_spmd, body=%wide.region_6.7_spmd.sunk | while | flops 787203 | bytes 273513 | solution.py:76
  421.8 16.3 %all-gather.6 = f32[8,1,256]{2,1,0:T(1,128)S(1)} all-gather(f32[1,1,256]{2,1,0:T(1,128)S(1)} %bitcast.199), channel_id=5, replica_groups=mesh['tm'=8,'exp'=4] {'tm'}, dimensions={0}, use_global_device_ids=true | all-gather | bytes 9216 | tf_op jit(solution)/shard_map/all_gather | solution.py:10
  438.1 10.8 %while.94 = (s32[]{:T(128)}, f32[256]{0:T(256)S(1)}, s32[]{:T(128)}, f32[8,256,256]{2,1,0:T(8,128)}, f32[8,256]{1,0:T(8,128)S(1)}, /*index=5*/s32[]{:T(128)}, s32[]{:T(128)}, s32[]{:T(128)}, s32[]{:T(128)}) while((s32[]{:T(128)}, f32[256]{0:T(256)S(1)}, s32[]{:T(128)}, f32[8,256,256]{2,1,0:T(8,128)}, f32[8,256]{1,0:T(8,128)S(1)}, ...), condition=%wide.region_9.10_spmd.clone, body=%wide.region_8.9_spmd.clone.sunk | while | flops 787464 | bytes 272552 | solution.py:21
  448.9 83.7 %while.91 = (s32[]{:T(128)}, f32[256]{0:T(256)S(1)}, f32[64,256]{1,0:T(8,128)S(1)}, f32[64,256]{1,0:T(8,128)S(1)}, f32[64,256]{1,0:T(8,128)S(1)}, /*index=5*/f32...) while((s32[]{:T(128)}, f32[256]{0:T(256)S(1)}, ...), condition=%wide.region_11.12_spmd, body=%wide.region_10.11_spmd.sunk | while | flops 787203 | bytes 278665 | solution.py:76
  533.7 76.5 %all-gather.15.cloned.1.call-done = f32[8192,256]{1,0:T(8,128)} async-done(((f32[256,256]{1,0:T(8,128)}), f32[8192,256]{1,0:T(8,128)}) %all-gather.15.cloned.1.call-update) | async-done | bytes 8388624 | tf_op jit(solution)/shard_map/all_gather | solution.py:108
  610.2 3.9 reduce_sum.9
  (1168 shorter events, 314.1 us)
Async XLA Ops:
  7.2 245.9 %copy-start = (f32[1,256]{1,0:T(1,128)S(1)}, f32[1,256]{1,0:T(1,128)}, u32[]{:S(2)}) copy-start(f32[1,256]{1,0:T(1,128)} %param.23) | copy-start | bytes 3076
  7.2 224.3 %all-gather.13.cloned.1.call-start = ((), (), s32[]{:S(2)}) async-start(), calls=%async_computation.1 | async-start | bytes 2359296 | tf_op jit(solution)/shard_map/all_gather | solution.py:10
  19.3 30.5 %copy-start.3 = (f32[1,64,256]{2,1,0:T(8,128)S(1)}, f32[1,64,256]{2,1,0:T(8,128)}, u32[]{:S(2)}) copy-start(f32[1,64,256]{2,1,0:T(8,128)} %param.22) | copy-start | bytes 196612
  19.3 30.5 %copy-start.4 = (s32[1,64,256]{2,1,0:T(8,128)S(1)}, s32[1,64,256]{2,1,0:T(8,128)}, u32[]{:S(2)}) copy-start(s32[1,64,256]{2,1,0:T(8,128)} %param.21) | copy-start | bytes 196612
  19.3 30.5 %copy-start.5 = (f32[256]{0:T(256)S(1)}, f32[256]{0:T(256)}, u32[]{:S(2)}) copy-start(f32[256]{0:T(256)} %param.24) | copy-start | bytes 3076
  86.6 5.2 copy-start.1
  91.8 346.3 %all-gather.11.cloned.1.call-start = ((), (), s32[]{:S(2)}) async-start(), calls=%async_computation | async-start | bytes 2359296 | tf_op jit(solution)/shard_map/all_gather | solution.py:10
  123.6 486.5 %all-gather.15.cloned.1.call-start = ((), (), s32[]{:S(2)}) async-start(), calls=%async_computation.2 | async-start | bytes 8650752 | tf_op jit(solution)/shard_map/all_gather | solution.py:108
  532.6 82.3 %copy-start.2 = (f32[64,256]{1,0:T(8,128)}, f32[64,256]{1,0:T(8,128)S(1)}, u32[]{:S(2)}) copy-start(f32[64,256]{1,0:T(8,128)S(1)} %get-tuple-element.599) | copy-start | bytes 196612
Sparse Core Ops, SparseCore 0:
  91.9 52.1 all-gather.12
  146.8 47.8 all-gather.10
  533.9 76.2 all-gather.14
